TPU v7x, 512 devices: a whole 4x4x16 slice. The times are simulated.
512 devices in a mesh: row: 64 (over z_lo, y, x), col: 8 (over z_hi, core).
Axes of the slice: x: 4, y: 4, z: 16 (z_hi: 4, z_lo: 4; z = z_hi * 4 + z_lo), core: 2. Of those that a mesh axis runs over, the one named last changes fastest.
Arguments:
- front: float32 [65536, 1024], P('row', 'col'), may hold values from -6 to 6
- contrib: bfloat16 [524288, 1024], P('row', 'col'), may hold values from -6 to 6
- target: int32 [2048], replicated, may hold values from 0 to 255, as said below
- mask: int32 [256, 8], P('row', 'col'), may hold values 0 or 1
- panel: float32 [65536, 256], P(('row', 'col')), as said below
- pivots: int32 [256], replicated, may hold values from 0 to 65535, as said below
Outputs:
- lower: float32 [65536, 256], P(('row', 'col'))
- schur: float32 [65536, 1024], P('row', 'col')
Inputs may be any that keep to these rules, and one draw needn't show every extreme that they name: Front block row t lies on index t // 4 of row. Within each aligned block of 32 entries (one device's contribution blocks) the values target // 4 are distinct, and index 0 of row receives a block from every aligned block. `pivots`: distinct rows; each aligned group of 1024 rows holds exactly 4 of them. The 256 x 256 matrix formed by the panel's rows named in pivots is invertible.
All inputs are finite; a program needn't handle non-finite values. No bound on the sum of `mask` on one device may be relied on, other than what follows from the above.
Results may differ from a plain program's by a relative error of at most 0.0003.
Values may be sent and summed in bfloat16 or wider, within the bound.
No kernel may reach another device: no remote copies, remote signals or barrier semaphores. Data moves between devices by JAX's collectives and lax.ppermute only.
A program may use at most 64 MiB of HBM per device.

v0:
```python
import jax
import jax.numpy as jnp
from jax import lax
from jax.sharding import PartitionSpec as P

BLK = 256


def exact_dot(left, right):
    return jnp.dot(left, right, precision=lax.Precision.HIGHEST, preferred_element_type=jnp.float32)


def body(front, contrib, target, mask, panel, pivots):
    row_count = lax.axis_size("row")
    col_count = lax.axis_size("col")
    row_index = lax.axis_index("row")
    col_index = lax.axis_index("col")
    tile_rows, tile_cols = front.shape
    blocks_own = tile_rows // BLK
    sent_count = contrib.shape[0] // BLK
    targets = target.reshape(row_count, sent_count)
    own_targets = lax.dynamic_slice_in_dim(targets, row_index, 1, 0)[0]
    device_ids = jnp.arange(row_count, dtype=jnp.int32)
    chooser = (own_targets[None, :] // blocks_own == device_ids[:, None]).astype(jnp.bfloat16)
    pieces = contrib.reshape(sent_count, BLK, tile_cols)
    outgoing = jnp.einsum(
        "db,bxc->dxc", chooser, pieces, preferred_element_type=jnp.float32
    ).astype(jnp.bfloat16)
    arrived = lax.all_to_all(outgoing, "row", split_axis=0, concat_axis=0, tiled=True)
    source_targets = jnp.take(targets, device_ids, axis=0)
    block_ids = jnp.arange(blocks_own, dtype=jnp.int32)
    own_blocks = row_index * blocks_own + block_ids
    placing = jnp.sum(
        (source_targets[:, :, None] == own_blocks[None, None, :]).astype(jnp.float32), axis=1
    ).astype(jnp.bfloat16)
    added = jnp.einsum("sk,sxc->kxc", placing, arrived, preferred_element_type=jnp.float32).reshape(
        tile_rows, tile_cols
    )
    assembled = front + added
    panel_rows = panel.shape[0]
    panel_start = (row_index * col_count + col_index) * panel_rows
    select_rows = (
        pivots[:, None] - panel_start == jnp.arange(panel_rows, dtype=jnp.int32)[None, :]
    ).astype(jnp.float32)
    pivot_block = lax.psum(exact_dot(select_rows, panel), ("row", "col"))
    gram = exact_dot(pivot_block, pivot_block.T)
    factor_low = jnp.linalg.cholesky(gram)
    inverse = jax.scipy.linalg.cho_solve((factor_low, True), pivot_block).T
    local_start = row_index * tile_rows
    picker = (
        pivots[:, None] - local_start == jnp.arange(tile_rows, dtype=jnp.int32)[None, :]
    ).astype(jnp.float32)
    upper = lax.psum(exact_dot(picker, assembled), "row")
    lower_own = exact_dot(panel, inverse)
    update = exact_dot(lax.all_gather(lower_own, "col", axis=0, tiled=True), upper)
    row_mask = jnp.repeat(mask[:, 0].astype(jnp.float32), BLK)
    schur = assembled - row_mask[:, None] * update
    return (lower_own, schur)


def solution(mesh):
    placed = (P("row", "col"), P("row", "col"), P(), P("row", "col"), P(("row", "col"), None), P())
    return jax.shard_map(
        body,
        mesh=mesh,
        in_specs=placed,
        out_specs=(P(("row", "col"), None), P("row", "col")),
        check_vma=False,
    )
```

profile of v0, /device:TPU:2, one launch (start us, length us, event | category | flops | bytes accessed | tf_op | source)
XLA Modules:
  0.0 1228.4 jit_solution(2532103232973570547)
XLA Ops:
  8.0 0.9 reshape.68
  8.9 0.7 copy-done
  9.6 1.8 convolution_convert_fusion
  11.4 4.7 copy.22
  16.1 12.4 %all-to-all-start = ((bf16[64,256,128]{2,1,0:T(8,128)(2,1)}), bf16[64,256,128]{2,1,0:T(8,128)(2,1)}, u32[]{:S(2)}, u32[]{:S(2)}) async-start(bf16[64,256,128]{2,1,0:T(8,128)(2,1)} %copy.22), calls=%async_computation | async-start | bytes 8388608 | tf_op jit(solution)/shard_map/all_to_all | solution.py:29
  28.5 0.0 all-reduce.4.cloned.1.call-start
  28.6 1.0 fusion.12
  29.6 0.0 all-reduce.4.cloned.1.call-update
  29.7 0.2 all-gather.2.cloned.1.call-start
  29.9 474.1 %all-reduce.4.cloned.1.call-done = f32[256,256]{1,0:T(8,128)} async-done(((f32[256,256]{1,0:T(8,128)}), f32[256,256]{1,0:T(8,128)}) %all-reduce.4.cloned.1.call-update) | async-done | bytes 262160 | tf_op jit(solution)/shard_map/psum | solution.py:45
  504.0 1.5 fusion.30
  505.5 0.1 copy.19
  505.7 11.7 cholesky.50
  517.5 9.8 custom-call.18
  527.3 0.2 constant_dynamic-update-slice_fusion
  527.5 0.3 convolution_subtract_fusion.2
  527.7 11.7 cholesky.105
  539.5 0.7 compare_reduce_fusion
  541.6 0.1 triangular_solve.66
  541.6 4.2 while.1
  541.8 0.6 fusion.46
  542.4 1.4 bitcast_dynamic-update-slice_fusion.2
  543.9 0.6 fusion.46
  544.5 1.4 bitcast_dynamic-update-slice_fusion.2
  545.9 0.6 copy-done.6
  546.5 20.5 %custom-call.19 = f32[2,128,128]{1,2,0:T(8,128)S(1)} custom-call(f32[2,128,128]{2,1,0:T(8,128)} %copy-done.6), custom_call_target="InvertDiagBlocksLowerTriangular" | custom-call | tf_op jit(solution)/shard_map/jit(_cho_solve)/triangular_solve | solution.py:48
  567.0 0.3 fusion.10
  567.4 0.3 convolution_subtract_fusion.1
  567.6 0.3 fusion.19
  568.0 0.3 fusion.18
  568.2 0.3 convolution_subtract_fusion
  568.5 0.3 fusion.17
  568.8 1.0 convolution_bitcast_fusion
  569.8 0.0 all-gather.2.cloned.1.call-update
  569.9 0.0 all-reduce.6.cloned.1.call-start
  569.9 0.6 gather_fusion
  570.6 0.1 broadcast_select_fusion
  570.6 0.1 copy.20
  570.7 0.1 convert_reduce_fusion
  570.8 4.5 fusion
  575.4 0.1 bitcast_add_fusion
  575.5 1.3 fusion.4
  576.8 0.0 all-reduce.6.cloned.1.call-update
  576.9 0.1 broadcast_bitcast_fusion
  576.9 0.8 copy.25
  577.7 41.3 %all-gather.2.cloned.1.call-done = f32[1024,256]{0,1:T(8,128)} async-done(((f32[128,256]{0,1:T(8,128)}), f32[1024,256]{0,1:T(8,128)}) %all-gather.2.cloned.1.call-update) | async-done | bytes 1048592 | tf_op jit(solution)/shard_map/all_gather | solution.py:55
  619.0 598.1 %all-reduce.6.cloned.1.call-done = f32[256,128]{1,0:T(8,128)} async-done(((f32[256,128]{1,0:T(8,128)}), f32[256,128]{1,0:T(8,128)}) %all-reduce.6.cloned.1.call-update) | async-done | bytes 131088 | tf_op jit(solution)/shard_map/psum | solution.py:53
  1217.1 3.9 fusion.3
  (34 shorter events, 0.3 us)
Async XLA Ops:
  8.0 1.6 copy-start
  16.1 12.5 %copy-start.5 = (s32[256]{0:T(256)S(1)}, s32[256]{0:T(256)}, u32[]{:S(2)}) copy-start(s32[256]{0:T(256)} %param.11) | copy-start | bytes 3076
  16.1 12.5 %copy-start.4 = (f32[128,256]{1,0:T(8,128)S(1)}, f32[128,256]{1,0:T(8,128)}, u32[]{:S(2)}) copy-start(f32[128,256]{1,0:T(8,128)} %param.10) | copy-start | bytes 393220
  16.1 554.7 %all-to-all-start = ((bf16[64,256,128]{2,1,0:T(8,128)(2,1)}), bf16[64,256,128]{2,1,0:T(8,128)(2,1)}, u32[]{:S(2)}, u32[]{:S(2)}) async-start(bf16[64,256,128]{2,1,0:T(8,128)(2,1)} %copy.22), calls=%async_computation | async-start | bytes 8388608 | tf_op jit(solution)/shard_map/all_to_all | solution.py:29
  28.5 475.4 %all-reduce.4.cloned.1.call-start = ((), (), s32[]{:S(2)}) async-start(), calls=%async_computation.1 | async-start | bytes 524288 | tf_op jit(solution)/shard_map/psum | solution.py:45
  29.6 541.2 %copy-start.7 = (s32[4,1]{0,1:T(1,128)S(1)}, s32[4,1]{0,1:T(1,128)}, u32[]{:S(2)}) copy-start(s32[4,1]{0,1:T(1,128)} %param.9) | copy-start | bytes 52
  29.7 589.3 %all-gather.2.cloned.1.call-start = ((), (), s32[]{:S(2)}) async-start(), calls=%async_computation.2 | async-start | bytes 1179648 | tf_op jit(solution)/shard_map/all_gather | solution.py:55
  504.0 63.1 %copy-start.1 = (f32[256,256]{1,0:T(8,128)S(1)}, f32[256,256]{1,0:T(8,128)}, u32[]{:S(2)}) copy-start(f32[256,256]{1,0:T(8,128)} %all-reduce.4.cloned.1.call-done) | copy-start | bytes 786436
  545.9 0.7 copy-start.6
  567.6 7.8 copy-start.3
  569.9 647.2 %all-reduce.6.cloned.1.call-start = ((), (), s32[]{:S(2)}) async-start(), calls=%async_computation.3 | async-start | bytes 262144 | tf_op jit(solution)/shard_map/psum | solution.py:53
  570.5 6.4 copy-start.2
Sparse Core Ops, SparseCore 0:
  35.4 468.5 all-reduce.3
  570.0 48.9 all-gather.1
Sparse Core Ops, SparseCore 1:
  576.9 640.1 all-reduce.5
where the time goes:
time: 1230 us
  waiting for transfers between devices  1110 us (90%)
  other arithmetic  54.8 us (4%)
  matrix products  17.3 us (1%)
  between operations  17.1 us (1%)
  local copies, waits for them, and re-layouts  12.7 us (1%)
  starting transfers between devices  12.7 us (1%)
    psum x1, waiting for transfers between devices, body(): upper = lax.psum(exact_dot(picker, assembled), 'row')  598 us
    psum x1, waiting for transfers between devices, body(): pivot_block = lax.psum(exact_dot(select_rows, panel), ('row', 'col'))  474 us
    all_gather x1, waiting for transfers between devices, body(): lax.all_gather(lower_own, 'col', axis=0, tiled=True)  41.3 us
    another operation x6, other arithmetic, body(): factor_low = jnp.linalg.cholesky(gram)  34 us
  transfers between devices with their start and end apart: 4, of which 3 were waited for; matrix products, arithmetic and copies ran while one was open for 6% of the time, Pallas kernels for 0%

commit v1 on v0

--- a/solution.py
+++ b/solution.py
@@ -4,6 +4,11 @@
 from jax.sharding import PartitionSpec as P
 
 BLK = 256
+
+
+def add_all(x, mesh_axis):
+    parts = lax.all_gather(x, mesh_axis)
+    return jnp.sum(parts, axis=0)
 
 
 def exact_dot(left, right):
@@ -50,7 +55,7 @@
     picker = (
         pivots[:, None] - local_start == jnp.arange(tile_rows, dtype=jnp.int32)[None, :]
     ).astype(jnp.float32)
-    upper = lax.psum(exact_dot(picker, assembled), "row")
+    upper = add_all(exact_dot(picker, assembled), "row")
     lower_own = exact_dot(panel, inverse)
     update = exact_dot(lax.all_gather(lower_own, "col", axis=0, tiled=True), upper)
     row_mask = jnp.repeat(mask[:, 0].astype(jnp.float32), BLK)

time: 1230 us -> 639 us (0.52)
  the two profiles are of different devices: /device:TPU:2 before, /device:TPU:97 now
where the time goes in v1:
time: 639 us; the launch traced here: 638 us
  waiting for transfers between devices  518 us (81%)
  other arithmetic  58.6 us (9%)
  matrix products  19 us (3%)
  between operations  17.1 us (3%)
  local copies, waits for them, and re-layouts  14.9 us (2%)
  starting transfers between devices  11 us (2%)
    psum x1, waiting for transfers between devices, body(): pivot_block = lax.psum(exact_dot(select_rows, panel), ('row', 'col'))  377 us
    all_to_all x1, waiting for transfers between devices, body(): lax.all_to_all(outgoing, 'row', split_axis=0, concat_axis=0, tiled=True)  90.4 us
    all_gather x1, waiting for transfers between devices, body(): lax.all_gather(lower_own, 'col', axis=0, tiled=True)  50.1 us
    another operation x6, other arithmetic, body(): factor_low = jnp.linalg.cholesky(gram)  34 us
    another operation x3, other arithmetic, body(): inverse = jax.scipy.linalg.cho_solve((factor_low, True), pivot_block).T  20.5 us
  transfers between devices with their start and end apart: 4, of which 3 were waited for; matrix products, arithmetic and copies ran while one was open for 13% of the time, Pallas kernels for 0%

profile of v1, /device:TPU:97, one launch (start us, length us, event | category | flops | bytes accessed | tf_op | source)
XLA Modules:
  0.0 638.5 jit_solution(16175735417411919406)
XLA Ops:
  8.0 0.9 reshape.68
  8.9 0.7 copy-done
  9.6 1.8 convolution_convert_fusion
  11.4 4.7 copy.22
  16.1 10.7 %all-to-all-start = ((bf16[64,256,128]{2,1,0:T(8,128)(2,1)}), bf16[64,256,128]{2,1,0:T(8,128)(2,1)}, u32[]{:S(2)}, u32[]{:S(2)}) async-start(bf16[64,256,128]{2,1,0:T(8,128)(2,1)} %copy.22), calls=%async_computation | async-start | bytes 8388608 | tf_op jit(solution)/shard_map/all_to_all | solution.py:34
  26.8 0.0 all-reduce.3.cloned.1.call-start
  26.9 1.0 fusion.12
  28.0 0.0 all-gather.6.cloned.1.call-start
  28.0 0.6 gather_fusion
  28.6 0.1 broadcast_select_fusion
  28.7 0.1 copy.20
  28.8 0.1 convert_reduce_fusion
  28.9 90.4 %all-to-all-done = bf16[64,256,128]{2,1,0:T(8,128)(2,1)} async-done(((bf16[64,256,128]{2,1,0:T(8,128)(2,1)}), bf16[64,256,128]{2,1,0:T(8,128)(2,1)}, u32[]{:S(2)}, u32[]{:S(2)}) %all-to-all-start) | async-done | bytes 4194336 | tf_op jit(solution)/shard_map/all_to_all | solution.py:34
  119.3 4.6 fusion
  123.9 0.1 bitcast_add_fusion
  123.9 1.3 fusion.4
  125.3 0.0 all-gather.6.cloned.1.call-update
  125.3 0.2 all-gather.4.cloned.1.call-start
  125.6 377.1 %all-reduce.3.cloned.1.call-done = f32[256,256]{1,0:T(8,128)} async-done(((f32[256,256]{1,0:T(8,128)}), f32[256,256]{1,0:T(8,128)}) %all-reduce.3.cloned.1.call-update) | async-done | bytes 262160 | tf_op jit(solution)/shard_map/psum | solution.py:50
  502.6 1.5 fusion.30
  504.2 0.1 copy.19
  504.4 0.7 copy-done.2
  505.1 11.7 %cholesky.50 = f32[128,128]{1,0:T(8,128)S(1)} custom-call(f32[128,128]{1,0:T(8,128)S(1)} %cholesky.118), custom_call_target="Cholesky" | custom-call | tf_op jit(solution)/shard_map/jit(cholesky)/cholesky | solution.py:52
  516.8 9.8 %custom-call.18 = f32[1,128,128]{1,2,0:T(8,128)S(1)} custom-call(f32[1,128,128]{2,1,0:T(8,128)S(1)} %get-tuple-element.31), custom_call_target="InvertDiagBlocksLowerTriangular" | custom-call | tf_op jit(solution)/shard_map/jit(cholesky)/cholesky | solution.py:52
  526.6 1.0 constant_dynamic-update-slice_fusion
  527.7 1.1 convolution_subtract_fusion.2
  528.8 11.7 %cholesky.105 = f32[128,128]{1,0:T(8,128)S(1)} custom-call(f32[128,128]{1,0:T(8,128)S(1)} %convolution_subtract_fusion.2), custom_call_target="Cholesky" | custom-call | tf_op jit(solution)/shard_map/jit(cholesky)/cholesky | solution.py:52
  540.6 0.7 compare_reduce_fusion
  542.6 0.1 triangular_solve.66
  542.7 5.5 while.1
  542.9 0.6 fusion.46
  543.5 2.0 bitcast_dynamic-update-slice_fusion.2
  545.5 0.6 fusion.46
  546.1 2.0 bitcast_dynamic-update-slice_fusion.2
  548.2 20.5 %custom-call.19 = f32[2,128,128]{1,2,0:T(8,128)S(1)} custom-call(f32[2,128,128]{2,1,0:T(8,128)} %get-tuple-element.9), custom_call_target="InvertDiagBlocksLowerTriangular" | custom-call | tf_op jit(solution)/shard_map/jit(_cho_solve)/triangular_solve | solution.py:53
  568.7 0.3 fusion.10
  569.0 0.3 convolution_subtract_fusion.1
  569.3 0.3 fusion.19
  569.6 0.3 fusion.18
  569.8 0.3 convolution_subtract_fusion
  570.2 0.3 fusion.17
  570.4 1.0 convolution_bitcast_fusion
  571.5 0.0 all-gather.4.cloned.1.call-update
  571.5 0.1 broadcast_bitcast_fusion
  571.6 1.7 copy.25
  573.3 3.8 reduce_sum.19
  577.0 50.1 %all-gather.4.cloned.1.call-done = f32[1024,256]{0,1:T(8,128)} async-done(((f32[128,256]{0,1:T(8,128)}), f32[1024,256]{0,1:T(8,128)}) %all-gather.4.cloned.1.call-update) | async-done | bytes 1048592 | tf_op jit(solution)/shard_map/all_gather | solution.py:60
  627.2 3.9 fusion.3
  (33 shorter events, 0.3 us)
Async XLA Ops:
  8.0 1.6 copy-start
  16.1 10.8 %copy-start.5 = (s32[256]{0:T(256)S(1)}, s32[256]{0:T(256)}, u32[]{:S(2)}) copy-start(s32[256]{0:T(256)} %param.11) | copy-start | bytes 3076
  16.1 10.8 %copy-start.4 = (f32[128,256]{1,0:T(8,128)S(1)}, f32[128,256]{1,0:T(8,128)}, u32[]{:S(2)}) copy-start(f32[128,256]{1,0:T(8,128)} %param.10) | copy-start | bytes 393220
  16.1 103.2 %all-to-all-start = ((bf16[64,256,128]{2,1,0:T(8,128)(2,1)}), bf16[64,256,128]{2,1,0:T(8,128)(2,1)}, u32[]{:S(2)}, u32[]{:S(2)}) async-start(bf16[64,256,128]{2,1,0:T(8,128)(2,1)} %copy.22), calls=%async_computation | async-start | bytes 8388608 | tf_op jit(solution)/shard_map/all_to_all | solution.py:34
  26.8 97.0 %copy-start.3 = (f32[1024,128]{1,0:T(8,128)S(1)}, f32[1024,128]{1,0:T(8,128)}, u32[]{:S(2)}) copy-start(f32[1024,128]{1,0:T(8,128)} %param.6) | copy-start | bytes 1572868
  26.8 475.8 %all-reduce.3.cloned.1.call-start = ((), (), s32[]{:S(2)}) async-start(), calls=%async_computation.1 | async-start | bytes 524288 | tf_op jit(solution)/shard_map/psum | solution.py:50
  28.0 545.3 %all-gather.6.cloned.1.call-start = ((), (), s32[]{:S(2)}) async-start(), calls=%async_computation.3 | async-start | bytes 8519680 | tf_op jit(solution)/shard_map/all_gather | solution.py:10
  123.9 447.6 %copy-start.6 = (s32[4,1]{0,1:T(1,128)S(1)}, s32[4,1]{0,1:T(1,128)}, u32[]{:S(2)}) copy-start(s32[4,1]{0,1:T(1,128)} %param.9) | copy-start | bytes 52
  125.3 501.9 %all-gather.4.cloned.1.call-start = ((), (), s32[]{:S(2)}) async-start(), calls=%async_computation.2 | async-start | bytes 1179648 | tf_op jit(solution)/shard_map/all_gather | solution.py:60
  502.6 66.0 %copy-start.1 = (f32[256,256]{1,0:T(8,128)S(1)}, f32[256,256]{1,0:T(8,128)}, u32[]{:S(2)}) copy-start(f32[256,256]{1,0:T(8,128)} %all-reduce.3.cloned.1.call-done) | copy-start | bytes 786436
  504.3 0.7 copy-start.2
Sparse Core Ops, SparseCore 0:
  33.7 468.9 all-reduce.2
Sparse Core Ops, SparseCore 1:
  125.4 294.7 all-gather.5
  571.6 55.5 all-gather.3
